TPU v7x, 256 devices: a whole 4x4x8 slice. The times are simulated.
256 devices in a mesh: row: 8 (over x, core), col: 32 (over z, y).
Axes of the slice: x: 4, y: 4, z: 8, core: 2. Of those that a mesh axis runs over, the one named last changes fastest.
Arguments:
- query_weight: float32 [16384, 16384], P('row', 'col'), may hold values from -6 to 6
Outputs:
- rotated: float32 [16384, 16384], P('row', 'col')
All inputs are finite; a program needn't handle non-finite values.
Results may differ from a plain program's by a relative error of at most 0.0001.
Values sent between devices are 32-bit elements; how exact they have to be, the bound alone decides.
A program may use at most 128 MiB of HBM per device.

v0:
```python
import jax
import jax.numpy as jnp
from jax import lax
from jax.sharding import PartitionSpec as P


def swapped(value, axis, bit):
    mask = 2**bit
    pairs = [(source, source ^ mask) for source in range(lax.axis_size(axis))]
    return lax.ppermute(value, axis, pairs)


def hadamard_table(length):
    rows_idx = lax.broadcasted_iota(jnp.int32, (length, length), 0)
    cols_idx = lax.broadcasted_iota(jnp.int32, (length, length), 1)
    common_bits = jnp.bitwise_and(rows_idx, cols_idx)
    parity = jnp.zeros((length, length), jnp.int32)
    for bit_pos in range(length.bit_length() - 1):
        parity = parity + jnp.bitwise_and(jnp.right_shift(common_bits, bit_pos), 1)
    return (1 - 2 * jnp.bitwise_and(parity, 1)).astype(jnp.float32)


def split_length(length):
    factors = []
    remain = length
    while remain > 128:
        factors.append(128)
        remain = remain // 128
    factors.append(remain)
    return factors


def transform_axis(values, along):
    factors = split_length(values.shape[along])
    shaped = values.reshape(values.shape[:along] + tuple(factors) + values.shape[along + 1 :])
    letters = "abcdefghij"
    rank_all = shaped.ndim
    for offset, factor in enumerate(factors):
        place = along + offset
        source = letters[:rank_all]
        target = source[:place] + "z" + source[place + 1 :]
        signs = hadamard_table(factor)
        shaped = jnp.einsum(
            "z" + source[place] + "," + source + "->" + target,
            signs,
            shaped,
            precision=lax.Precision.HIGHEST,
        )
    return shaped.reshape(values.shape)


def per_device(query_weight):
    rows_local = query_weight.shape[0]
    cols_local = query_weight.shape[1]
    n_row = lax.axis_size("row")
    n_col = lax.axis_size("col")
    norm_factor = 1.0 / (rows_local * n_row)
    sub_rows = rows_local // n_col
    current = transform_axis(query_weight, 0)
    own_index = lax.axis_index("row")
    for bit_pos in range(n_row.bit_length() - 1):
        partner = swapped(current, "row", bit_pos)
        high_half = jnp.bitwise_and(jnp.right_shift(own_index, bit_pos), 1) == 1
        current = jnp.where(high_half, partner - current, current + partner)
    stacked = current.reshape(n_col, sub_rows, cols_local)
    turned = (
        transform_axis(lax.all_to_all(stacked, "col", split_axis=0, concat_axis=2, tiled=True), 2)
        * norm_factor
    )
    result = lax.all_to_all(turned, "col", split_axis=2, concat_axis=0, tiled=True)
    return result.reshape(rows_local, cols_local)


def solution(mesh):
    in_specs = (P("row", "col"),)
    out_specs = P("row", "col")
    return jax.shard_map(
        per_device, mesh=mesh, in_specs=in_specs, out_specs=out_specs, check_vma=False
    )
```

profile of v0, /device:TPU:12, one launch (start us, length us, event | category | flops | bytes accessed | tf_op | source)
XLA Modules:
  0.0 583.0 jit_solution(5615847860724308181)
XLA Ops:
  0.0 8.2 %fusion.4 = f32[128,16,512]{2,0,1:T(8,128)S(1)} fusion(f32[128,16,512]{2,1,0:T(8,128)} %bitcast.42), kind=kOutput, calls=%fused_computation.4 | convolution fusion | flops 1611022336 | bytes 8388608 | tf_op jit(solution)/shard_map/za,abc->zbc/dot_general | solution.py:43
  8.2 6.7 %fusion.2 = f32[128,512,16]{1,2,0:T(8,128)} fusion(f32[128,16,512]{2,0,1:T(8,128)S(1)} %fusion.4), kind=kOutput, calls=%fused_computation.2 | convolution fusion | flops 201330688 | bytes 8388608 | tf_op jit(solution)/shard_map/zb,abc->azc/dot_general | solution.py:43
  14.9 0.0 collective-permute-start
  14.9 7.5 %collective-permute-done = f32[2048,512]{1,0:T(8,128)} collective-permute-done((f32[2048,512]{1,0:T(8,128)}, f32[2048,512]{1,0:T(8,128)}, u32[]{:S(2)}, u32[]{:S(2)}) %collective-permute-start) | collective-permute-done | bytes 4194336 | tf_op jit(solution)/shard_map/ppermute | solution.py:10
  22.4 6.4 %add_select_fusion.2 = f32[2048,512]{1,0:T(8,128)} fusion(f32[2048,512]{1,0:T(8,128)} %collective-permute-done, pred[]{:T(512)S(6)} %eq.11, f32[128,512,16]{1,2,0:T(8,128)} %fusion.2), kind=kLoop, calls=%fused_computation.8 | loop fusion | flops 3145728 | bytes 12582913 | tf_op jit(solution)/shard_map/jit(_where)/select_n | solution.py:64
  28.8 1.2 collective-permute-start.1
  30.0 91.7 %collective-permute-done.1 = f32[2048,512]{1,0:T(8,128)} collective-permute-done((f32[2048,512]{1,0:T(8,128)}, f32[2048,512]{1,0:T(8,128)}, u32[]{:S(2)}, u32[]{:S(2)}) %collective-permute-start.1) | collective-permute-done | bytes 4194336 | tf_op jit(solution)/shard_map/ppermute | solution.py:10
  121.8 6.5 %add_select_fusion.1 = f32[2048,512]{1,0:T(8,128)} fusion(f32[2048,512]{1,0:T(8,128)} %add_select_fusion.2, f32[2048,512]{1,0:T(8,128)} %collective-permute-done.1, pred[]{:T(512)S(6)} %eq.10), kind=kLoop, calls=%fused_computation.7 | loop fusion | flops 3145728 | bytes 12582913 | tf_op jit(solution)/shard_map/jit(_where)/select_n | solution.py:64
  128.3 0.5 collective-permute-start.2
  128.8 93.1 %collective-permute-done.2 = f32[2048,512]{1,0:T(8,128)} collective-permute-done((f32[2048,512]{1,0:T(8,128)}, f32[2048,512]{1,0:T(8,128)}, u32[]{:S(2)}, u32[]{:S(2)}) %collective-permute-start.2) | collective-permute-done | bytes 4194336 | tf_op jit(solution)/shard_map/ppermute | solution.py:10
  221.9 4.5 add_select_fusion
  226.4 105.6 %all_to_all.30 = f32[32,64,512]{2,1,0:T(8,128)S(1)} all-to-all(f32[32,64,512]{2,1,0:T(8,128)S(1)} %bitcast.40), channel_id=1, replica_groups=mesh['row'=8,'col'=32] {'col'}, dimensions={0} | all-to-all | bytes 8388608 | tf_op jit(solution)/shard_map/all_to_all | solution.py:67
  331.9 4.4 copy.15
  336.4 4.7 reshape.43
  341.1 8.6 %fusion.10 = f32[64,128,128]{2,1,0:T(8,128)S(1)} fusion(f32[64,128,128]{2,1,0:T(8,128)} %reshape.43), kind=kOutput, calls=%fused_computation.11 | convolution fusion | flops 1611022336 | bytes 8388608 | tf_op jit(solution)/shard_map/zc,abcd->abzd/dot_general | solution.py:43
  349.7 8.3 %fusion.6 = f32[64,128,128]{2,1,0:T(8,128)} fusion(f32[64,128,128]{2,1,0:T(8,128)S(1)} %fusion.10), kind=kOutput, calls=%fused_computation.9 | convolution fusion | flops 1612070912 | bytes 8388608 | tf_op jit(solution)/shard_map/zd,abcd->abcz/dot_general | solution.py:43
  358.0 7.0 %copy.22 = f32[64,128,128]{0,2,1:T(8,128)} copy(f32[64,128,128]{2,1,0:T(8,128)} %fusion.6) | data formatting | bytes 8388608 | tf_op jit(solution)/shard_map/mul | solution.py:67
  365.0 0.5 broadcast.124
  365.5 74.6 %reduce = f32[16384,64]{1,0:T(8,128)} reduce(f32[16384,1,64]{2,1,0:T(1,128)} %bitcast.38, f32[]{:T(128)} %broadcast.124), dimensions={1}, to_apply=%bitcast.35.reduce_sub_computation | reduce | bytes 8388612
  440.1 9.8 %reshape.48 = f32[32,1,32768]{2,1,0:T(1,128)} reshape(f32[16384,64]{1,0:T(8,128)} %reduce) | data formatting | bytes 8388608
  449.9 99.6 %all_to_all.31 = f32[32,1,32768]{2,1,0:T(1,128)} all-to-all(f32[32,1,32768]{2,1,0:T(1,128)} %reshape.48), channel_id=1, replica_groups=mesh['row'=8,'col'=32] {'col'}, dimensions={0} | all-to-all | bytes 8388608 | tf_op jit(solution)/shard_map/all_to_all | solution.py:70
  549.5 13.7 %reduce.1 = f32[32,32768]{1,0:T(8,128)} reduce(f32[32,1,32768]{2,1,0:T(1,128)} %all_to_all.31, f32[]{:T(128)} %broadcast.124), dimensions={1}, to_apply=%all_to_all.25.reduce_sub_computation | reduce | bytes 8388612 | tf_op jit(solution)/shard_map/all_to_all | solution.py:70
  563.1 13.1 %reshape.49 = f32[16384,1,64]{2,1,0:T(1,128)} reshape(f32[32,32768]{1,0:T(8,128)} %reduce.1) | data formatting | bytes 8388608
  576.2 6.8 %copy.19 = f32[32,1,64,512]{3,2,0,1:T(8,128)} copy(f32[32,1,64,512]{2,3,0,1:T(8,128)} %bitcast.39) | data formatting | bytes 8388608 | tf_op jit(solution)/shard_map/all_to_all | solution.py:70
Async XLA Ops:
  14.9 7.5 %collective-permute-start = (f32[2048,512]{1,0:T(8,128)}, f32[2048,512]{1,0:T(8,128)}, u32[]{:S(2)}, u32[]{:S(2)}) collective-permute-start(f32[2048,512]{1,0:T(8,128)} %bitcast.4), channel_id=1, source_target_pairs={{0,32},{32,0},{64,96},{96,64},{128,160},{160,128},{192,224},{224,1... | collective-permute-start | bytes 12582920 | tf_op jit(solution)/shard_map/ppermute | solution.py:10
  28.8 92.9 %collective-permute-start.1 = (f32[2048,512]{1,0:T(8,128)}, f32[2048,512]{1,0:T(8,128)}, u32[]{:S(2)}, u32[]{:S(2)}) collective-permute-start(f32[2048,512]{1,0:T(8,128)} %add_select_fusion.2), channel_id=1, source_target_pairs={{0,64},{32,96},{64,0},{96,32},{128,192},{160,224},{192,128},{224,1... | collective-permute-start | bytes 12582920 | tf_op jit(solution)/shard_map/ppermute | solution.py:10
  128.3 93.6 %collective-permute-start.2 = (f32[2048,512]{1,0:T(8,128)}, f32[2048,512]{1,0:T(8,128)}, u32[]{:S(2)}, u32[]{:S(2)}) collective-permute-start(f32[2048,512]{1,0:T(8,128)} %add_select_fusion.1), channel_id=1, source_target_pairs={{0,128},{32,160},{64,192},{96,224},{128,0},{160,32},{192,64},{224,... | collective-permute-start | bytes 12582920 | tf_op jit(solution)/shard_map/ppermute | solution.py:10
where the time goes:
time: 584 us; the launch traced here: 583 us
  blocking collectives  205 us (35%)
  waiting for transfers between devices  192 us (33%)
  other arithmetic  106 us (18%)
  local copies, waits for them, and re-layouts  46.3 us (8%)
  matrix products  31.8 us (5%)
    ppermute x3, waiting for transfers between devices, swapped(): return lax.ppermute(value, axis, pairs)  192 us
    all_to_all x1, blocking collectives, per_device(): lax.all_to_all(stacked, 'col', split_axis=0, concat_axis=2, tiled=True)  106 us
    all_to_all x1, blocking collectives, per_device(): lax.all_to_all(turned, 'col', split_axis=2, concat_axis=0, tiled=True)  99.6 us
    unnamed x1, other arithmetic  74.6 us
    dot_general x4, matrix products, transform_axis(): jnp.einsum('z' + source[place] + ',' + source + '->' + target, signs, sha...  31.8 us
    unnamed x3, local copies, waits for them, and re-layouts  23.4 us
    select_n x3, other arithmetic, per_device(): current = jnp.where(high_half, partner - current, current + partner)  17.5 us
    all_to_all x1, other arithmetic, per_device(): lax.all_to_all(turned, 'col', split_axis=2, concat_axis=0, tiled=True)  13.7 us
  transfers between devices with their start and end apart: 3, of which 3 were waited for; matrix products, arithmetic and copies ran while one was open for 0% of the time, Pallas kernels for 0%

commit v1 on v0

v1 whole, which is shorter than its diff:
```python
import functools

import jax
import jax.numpy as jnp
from jax import lax
from jax.experimental import pallas as pl
from jax.experimental.pallas import tpu as pltpu
from jax.sharding import PartitionSpec as P

MESH = pl.DeviceIdType.MESH
LANES = 128
CHUNKS = 4
Z_ORDER = (1, 7, 2, 6, 3, 5, 4)


def butterfly(values):
    values = list(values)
    half = 1
    while half < len(values):
        for base in range(0, len(values), 2 * half):
            for i in range(base, base + half):
                low, high = values[i], values[i + half]
                values[i], values[i + half] = low + high, low - high
        half *= 2
    return values


def signs(rows, cols):
    i = lax.broadcasted_iota(jnp.int32, (rows, cols), 0)
    j = lax.broadcasted_iota(jnp.int32, (rows, cols), 1)
    bits = jnp.bitwise_and(i, j)
    for shift in (8, 4, 2, 1):
        bits = jnp.bitwise_xor(bits, jnp.right_shift(bits, shift))
    return (1 - 2 * jnp.bitwise_and(bits, 1)).astype(jnp.float32).astype(jnp.bfloat16)


def split(value):
    high = value.astype(jnp.bfloat16)
    low = (value - high.astype(jnp.float32)).astype(jnp.bfloat16)
    return high, low


def exchange_kernel(n_z, n_y, n_row, x_ref, a_out, b_out, z_in, z_sum, z_back, p_in, p_sum, p_back, local, table, send_sem, recv_sem, out_sem):
    row = lax.axis_index("row")
    col = lax.axis_index("col")
    z = col // n_y
    y = lax.rem(col, n_y)
    n_p = n_row * n_y
    p = row * n_y + y
    blocks, lanes = x_ref.shape[1], x_ref.shape[3]
    z_len, p_len = blocks // n_z, blocks // n_p

    def z_peer(step):
        k = lax.rem(z + step, n_z)
        return k, (row, k * n_y + y)

    def p_peer(step):
        k = lax.rem(p + step, n_p)
        return k, (k // n_y, z * n_y + lax.rem(k, n_y))

    barrier = pltpu.get_barrier_semaphore()
    for step in Z_ORDER:
        pl.semaphore_signal(barrier, inc=1, device_id=z_peer(step)[1], device_id_type=MESH)

    @pl.loop(1, n_p)
    def _(step):
        pl.semaphore_signal(barrier, inc=1, device_id=p_peer(step)[1], device_id_type=MESH)

    pl.semaphore_wait(barrier, n_z - 1 + n_p - 1)

    def z_send(src, dst, slot):
        mine = pl.ds(z * z_len, z_len)
        for step in Z_ORDER:
            k, device = z_peer(step)
            pltpu.make_async_remote_copy(
                src_ref=src.at[pl.ds(k * z_len, z_len)], dst_ref=dst.at[mine],
                send_sem=send_sem.at[slot], recv_sem=recv_sem.at[slot], device_id=device, device_id_type=MESH,
            ).start()
        pltpu.make_async_copy(src.at[mine], dst.at[mine], recv_sem.at[slot]).start()

    def p_send(src, dst, slot):
        mine = pl.ds(p * p_len, p_len)

        @pl.loop(1, n_p)
        def _(step):
            k, device = p_peer(step)
            pltpu.make_async_remote_copy(
                src_ref=src.at[pl.ds(k * p_len, p_len)], dst_ref=dst.at[mine],
                send_sem=send_sem.at[slot], recv_sem=recv_sem.at[slot], device_id=device, device_id_type=MESH,
            ).start()

        pltpu.make_async_copy(src.at[mine], dst.at[mine], recv_sem.at[slot]).start()

    def arrived(dst, slot):
        pltpu.make_async_copy(dst, dst, recv_sem.at[slot]).wait()

    def sent(ref, length, slot):
        part = ref.at[pl.ds(0, blocks - length)]
        pltpu.make_async_copy(part, part, send_sem.at[slot]).wait()

    def combine(src, dst, count, length):
        @pl.loop(0, length)
        def _(t):
            for lane in range(0, lanes, LANES):
                at = slice(lane, lane + LANES)
                done = butterfly([src[k * length + t, :, at] for k in range(count)])
                for k in range(count):
                    dst[k * length + t, :, at] = done[k]

    def transform(src, dst):
        size = 256
        groups = blocks * 8 // size
        step_blocks = size // 8

        @pl.loop(0, 2 * groups)
        def _(g):
            chunk, part = g // groups, lax.rem(g, groups)
            at = pl.ds(part * step_blocks, step_blocks)
            high, low = split(src[chunk, at].reshape(size, lanes))
            wide = table[...]
            value = jnp.dot(high, wide, preferred_element_type=jnp.float32) + jnp.dot(low, wide, preferred_element_type=jnp.float32)
            high, low = split(value)
            tall = table[0:size, 0:size]
            value = jnp.dot(tall, high, preferred_element_type=jnp.float32) + jnp.dot(tall, low, preferred_element_type=jnp.float32)
            dst[chunk, at] = value.reshape(step_blocks, 8, lanes)

        @pl.loop(0, step_blocks)
        def _(t):
            for lane in range(0, lanes, LANES):
                at = slice(lane, lane + LANES)
                places = [(chunk, part * step_blocks) for chunk in range(2) for part in range(groups)]
                done = butterfly([dst[chunk, base + t, :, at] for chunk, base in places])
                for (chunk, base), value in zip(places, done):
                    dst[chunk, base + t, :, at] = value

    a_chunks, b_chunks = (0, 1), (2, 3)
    for a, b in zip(a_chunks, b_chunks):
        z_send(x_ref.at[a], z_in.at[a], a)
        p_send(x_ref.at[b], p_in.at[b], 8 + b)

    table[...] = signs(lanes, lanes)

    for a, b in zip(a_chunks, b_chunks):
        arrived(p_in.at[b], 8 + b)
        combine(p_in.at[b], p_sum.at[b], n_p, p_len)
        p_send(p_sum.at[b], p_back.at[b], 12 + b)
        arrived(z_in.at[a], a)
        combine(z_in.at[a], z_sum.at[a], n_z, z_len)
        z_send(z_sum.at[a], z_back.at[a], 4 + a)

    for b in b_chunks:
        arrived(p_back.at[b], 12 + b)
    transform(p_back.at[pl.ds(2, 2)], local.at[pl.ds(2, 2)])
    for b in b_chunks:
        z_send(local.at[b], z_in.at[b], b)

    for a in a_chunks:
        arrived(z_back.at[a], 4 + a)
        p_send(z_back.at[a], p_in.at[a], 8 + a)
    for a in a_chunks:
        arrived(p_in.at[a], 8 + a)
        combine(p_in.at[a], p_sum.at[a], n_p, p_len)
        p_send(p_sum.at[a], p_back.at[a], 12 + a)

    arrived(z_in.at[2], 2)
    combine(z_in.at[2], z_sum.at[2], n_z, z_len)
    z_send(z_sum.at[2], b_out.at[0], 6)

    for a in a_chunks:
        arrived(p_back.at[a], 12 + a)
    transform(p_back.at[pl.ds(0, 2)], local.at[pl.ds(0, 2)])
    pltpu.make_async_copy(local.at[pl.ds(0, 2)], a_out, out_sem).start()

    arrived(z_in.at[3], 3)
    combine(z_in.at[3], z_sum.at[3], n_z, z_len)
    z_send(z_sum.at[3], b_out.at[1], 7)

    for b in b_chunks:
        arrived(b_out.at[b - 2], 4 + b)
    pltpu.make_async_copy(local.at[pl.ds(0, 2)], a_out, out_sem).wait()
    for c in range(CHUNKS):
        sent(z_in.at[c], z_len, c)
        sent(z_in.at[c], z_len, 4 + c)
        sent(p_in.at[c], p_len, 8 + c)
        sent(p_in.at[c], p_len, 12 + c)


def mix_kernel(scale, a_ref, b_ref, o_ref):
    a, b = a_ref[...], b_ref[...]
    o_ref[0] = (a + b) * scale
    o_ref[1] = (a - b) * scale


def per_device(n_z, n_y, n_row, scale, query_weight):
    rows, lanes = query_weight.shape
    blocks = rows // CHUNKS // 8
    x = query_weight.reshape(CHUNKS, blocks, 8, lanes)
    half = jax.ShapeDtypeStruct((2, blocks, 8, lanes), jnp.float32)
    full = pltpu.VMEM((CHUNKS, blocks, 8, lanes), jnp.float32)
    anywhere = pl.BlockSpec(memory_space=pl.ANY)
    a, b = pl.pallas_call(
        functools.partial(exchange_kernel, n_z, n_y, n_row),
        out_shape=(half, half),
        in_specs=[anywhere],
        out_specs=(anywhere, anywhere),
        scratch_shapes=[
            full, full, pltpu.VMEM((2, blocks, 8, lanes), jnp.float32), full, full, full, full,
            pltpu.VMEM((lanes, lanes), jnp.bfloat16),
            pltpu.SemaphoreType.DMA((4 * CHUNKS,)), pltpu.SemaphoreType.DMA((4 * CHUNKS,)), pltpu.SemaphoreType.DMA,
        ],
        compiler_params=pltpu.CompilerParams(collective_id=0, has_side_effects=True, vmem_limit_bytes=60 * 2**20),
        name="exchange",
    )(x)
    steps = 4
    tall = rows // 2 // steps
    a, b = a.reshape(rows // 2, lanes), b.reshape(rows // 2, lanes)
    out = pl.pallas_call(
        functools.partial(mix_kernel, scale),
        out_shape=jax.ShapeDtypeStruct((2, rows // 2, lanes), jnp.float32),
        grid=(steps,),
        in_specs=[pl.BlockSpec((tall, lanes), lambda i: (i, 0))] * 2,
        out_specs=pl.BlockSpec((2, tall, lanes), lambda i: (0, i, 0)),
        name="mix",
    )(a, b)
    return out.reshape(rows, lanes)


def solution(mesh):
    n_row, n_col = mesh.shape["row"], mesh.shape["col"]
    n_y = 4
    n_z = n_col // n_y

    def run(query_weight):
        scale = 1.0 / query_weight.shape[0]
        body = functools.partial(per_device, n_z, n_y, n_row, scale)
        return jax.shard_map(body, mesh=mesh, in_specs=(P("row", "col"),), out_specs=P("row", "col"), check_vma=False)(query_weight)

    return run
```

time: 584 us -> 199 us (0.34)
  blocking collectives: 205 us -> 0 us
  Pallas kernels: 0 us -> 195 us
  waiting for transfers between devices: 192 us -> 0 us
  other arithmetic: 106 us -> 0 us
  local copies, waits for them, and re-layouts: 46.3 us -> 0 us
  matrix products: 31.8 us -> 0 us
    all_to_all x2 -> x0, blocking collectives: 205 us -> none  [the longest x1 106 us: per_device(): lax.all_to_all(stacked, 'col', split_axis=0, concat_axis=2, tiled=True)]
    pallas_call x0 -> x2, Pallas kernels: none -> 195 us  [the longest x1 191 us: per_device(): pl.pallas_call(functools.partial(exchange_kernel, n_z, n_y, n_row), out_s...]
    ppermute x3 -> x0, waiting for transfers between devices: 192 us -> none  [swapped(): return lax.ppermute(value, axis, pairs)]
    unnamed x1 -> x0, other arithmetic: 74.6 us -> none
    dot_general x4 -> x0, matrix products: 31.8 us -> none  [transform_axis(): jnp.einsum('z' + source[place] + ',' + source + '->' + target, signs, sha...]
    unnamed x3 -> x0, local copies, waits for them, and re-layouts: 23.4 us -> none
    select_n x3 -> x0, other arithmetic: 17.5 us -> none  [per_device(): current = jnp.where(high_half, partner - current, current + partner)]
    all_to_all x1 -> x0, other arithmetic: 13.7 us -> none  [per_device(): lax.all_to_all(turned, 'col', split_axis=2, concat_axis=0, tiled=True)]
  transfers between devices with their start and end apart: 3 -> 0, of which waited for: 3 -> 0; matrix products, arithmetic and copies ran while one was open for 0% -> 0% of each run, Pallas kernels for 0% -> 0%
where the time goes in v1:
time: 199 us; the launch traced here: 195 us
  Pallas kernels  195 us (98%)
    pallas_call x1, Pallas kernels, per_device(): pl.pallas_call(functools.partial(exchange_kernel, n_z, n_y, n_row), out_s...  191 us
    pallas_call x1, Pallas kernels, per_device(): pl.pallas_call(functools.partial(mix_kernel, scale), out_shape=jax.ShapeD...  4.77 us

profile of v1, /device:TPU:12, one launch (start us, length us, event | category | flops | bytes accessed | tf_op | source)
XLA Modules:
  0.0 195.3 jit_solution(14116001480194307679)
XLA Ops:
  0.0 190.6 %exchange.1 = (f32[2,64,8,512]{3,2,1,0:T(8,128)}, f32[2,64,8,512]{3,2,1,0:T(8,128)}) custom-call(f32[4,64,8,512]{3,2,1,0:T(8,128)} %bitcast.4), custom_call_target="tpu_custom_call" | custom-call | tf_op jit(solution)/shard_map/exchange/pallas_call | solution.py:201
  190.6 4.8 %mix.1 = f32[2,1024,512]{2,1,0:T(8,128)} custom-call(f32[1024,512]{1,0:T(8,128)} %bitcast.5, f32[1024,512]{1,0:T(8,128)} %bitcast.6), custom_call_target="tpu_custom_call" | custom-call | tf_op jit(solution)/shard_map/mix/pallas_call | solution.py:217

commit v2 on v1

--- a/solution.py
+++ b/solution.py
@@ -10,7 +10,7 @@
 MESH = pl.DeviceIdType.MESH
 LANES = 128
 CHUNKS = 4
-Z_ORDER = (1, 7, 2, 6, 3, 5, 4)
+Z_ORDER = (4, 3, 5, 2, 6, 1, 7)
 
 
 def butterfly(values):
@@ -40,7 +40,7 @@
     return high, low
 
 
-def exchange_kernel(n_z, n_y, n_row, x_ref, a_out, b_out, z_in, z_sum, z_back, p_in, p_sum, p_back, local, table, send_sem, recv_sem, out_sem):
+def exchange_kernel(n_z, n_y, n_row, x_ref, a_out, b_out, z_in, z_sum, z_back, p_in, p_sum, p_back, local, table, send_sem, recv_sem):
     row = lax.axis_index("row")
     col = lax.axis_index("col")
     z = col // n_y
@@ -150,9 +150,9 @@
 
     for b in b_chunks:
         arrived(p_back.at[b], 12 + b)
-    transform(p_back.at[pl.ds(2, 2)], local.at[pl.ds(2, 2)])
+    transform(p_back.at[pl.ds(2, 2)], local)
     for b in b_chunks:
-        z_send(local.at[b], z_in.at[b], b)
+        z_send(local.at[b - 2], z_in.at[b], b)
 
     for a in a_chunks:
         arrived(z_back.at[a], 4 + a)
@@ -168,8 +168,7 @@
 
     for a in a_chunks:
         arrived(p_back.at[a], 12 + a)
-    transform(p_back.at[pl.ds(0, 2)], local.at[pl.ds(0, 2)])
-    pltpu.make_async_copy(local.at[pl.ds(0, 2)], a_out, out_sem).start()
+    transform(p_back.at[pl.ds(0, 2)], a_out)
 
     arrived(z_in.at[3], 3)
     combine(z_in.at[3], z_sum.at[3], n_z, z_len)
@@ -177,7 +176,6 @@
 
     for b in b_chunks:
         arrived(b_out.at[b - 2], 4 + b)
-    pltpu.make_async_copy(local.at[pl.ds(0, 2)], a_out, out_sem).wait()
     for c in range(CHUNKS):
         sent(z_in.at[c], z_len, c)
         sent(z_in.at[c], z_len, 4 + c)
@@ -185,41 +183,51 @@
         sent(p_in.at[c], p_len, 12 + c)
 
 
-def mix_kernel(scale, a_ref, b_ref, o_ref):
-    a, b = a_ref[...], b_ref[...]
-    o_ref[0] = (a + b) * scale
-    o_ref[1] = (a - b) * scale
+def mix_kernel(scale, steps, a_ref, b_ref, o_ref, plus, minus, sem):
+    chunks, blocks = a_ref.shape[:2]
+    size = chunks * blocks // steps
+    copies = []
+    for i in range(steps):
+        chunk, at = i * size // blocks, pl.ds(i * size % blocks, size)
+        a, b = a_ref[chunk, at], b_ref[chunk, at]
+        plus[chunk, at] = (a + b) * scale
+        minus[chunk, at] = (a - b) * scale
+        for half, made in enumerate((plus, minus)):
+            copies.append(pltpu.make_async_copy(made.at[chunk, at], o_ref.at[half, chunk, at], sem.at[half, i]))
+            copies[-1].start()
+    for copy in copies:
+        copy.wait()
 
 
 def per_device(n_z, n_y, n_row, scale, query_weight):
     rows, lanes = query_weight.shape
     blocks = rows // CHUNKS // 8
     x = query_weight.reshape(CHUNKS, blocks, 8, lanes)
-    half = jax.ShapeDtypeStruct((2, blocks, 8, lanes), jnp.float32)
+    half = pltpu.VMEM((2, blocks, 8, lanes), jnp.float32)
     full = pltpu.VMEM((CHUNKS, blocks, 8, lanes), jnp.float32)
     anywhere = pl.BlockSpec(memory_space=pl.ANY)
     a, b = pl.pallas_call(
         functools.partial(exchange_kernel, n_z, n_y, n_row),
         out_shape=(half, half),
-        in_specs=[anywhere],
-        out_specs=(anywhere, anywhere),
+        in_specs=[pl.BlockSpec(memory_space=pltpu.HBM)],
+        out_specs=(pl.BlockSpec(memory_space=pltpu.VMEM),) * 2,
         scratch_shapes=[
-            full, full, pltpu.VMEM((2, blocks, 8, lanes), jnp.float32), full, full, full, full,
+            full, full, half, full, full, full, half,
             pltpu.VMEM((lanes, lanes), jnp.bfloat16),
-            pltpu.SemaphoreType.DMA((4 * CHUNKS,)), pltpu.SemaphoreType.DMA((4 * CHUNKS,)), pltpu.SemaphoreType.DMA,
+            pltpu.SemaphoreType.DMA((4 * CHUNKS,)), pltpu.SemaphoreType.DMA((4 * CHUNKS,)),
         ],
-        compiler_params=pltpu.CompilerParams(collective_id=0, has_side_effects=True, vmem_limit_bytes=60 * 2**20),
+        compiler_params=pltpu.CompilerParams(collective_id=0, has_side_effects=True, vmem_limit_bytes=58 * 2**20),
         name="exchange",
     )(x)
-    steps = 4
-    tall = rows // 2 // steps
-    a, b = a.reshape(rows // 2, lanes), b.reshape(rows // 2, lanes)
+    steps = 8
+    a, b = (pltpu.with_memory_space_constraint(part, pltpu.VMEM) for part in (a, b))
     out = pl.pallas_call(
-        functools.partial(mix_kernel, scale),
-        out_shape=jax.ShapeDtypeStruct((2, rows // 2, lanes), jnp.float32),
-        grid=(steps,),
-        in_specs=[pl.BlockSpec((tall, lanes), lambda i: (i, 0))] * 2,
-        out_specs=pl.BlockSpec((2, tall, lanes), lambda i: (0, i, 0)),
+        functools.partial(mix_kernel, scale, steps),
+        out_shape=jax.ShapeDtypeStruct((2, *half.shape), jnp.float32),
+        in_specs=[pl.BlockSpec(memory_space=pltpu.VMEM)] * 2,
+        out_specs=anywhere,
+        scratch_shapes=[half, half, pltpu.SemaphoreType.DMA((2, steps))],
+        compiler_params=pltpu.CompilerParams(vmem_limit_bytes=16 * 2**20),
         name="mix",
     )(a, b)
     return out.reshape(rows, lanes)

time: 199 us -> 196 us (0.985)
  Pallas kernels: 195 us -> 193 us
    pallas_call x1, Pallas kernels: 4.77 us -> 2.17 us  [per_device(): pl.pallas_call(functools.partial(mix_kernel, scale, steps), out_shape=jax...]
where the time goes in v2:
time: 196 us; the launch traced here: 193 us
  Pallas kernels  193 us (98%)
    pallas_call x1, Pallas kernels, per_device(): pl.pallas_call(functools.partial(exchange_kernel, n_z, n_y, n_row), out_s...  191 us

profile of v2, /device:TPU:12, one launch (start us, length us, event | category | flops | bytes accessed | tf_op | source)
XLA Modules:
  0.0 192.8 jit_solution(8693969231513019804)
XLA Ops:
  0.0 190.6 %exchange.1 = (f32[2,64,8,512]{3,2,1,0:T(8,128)S(1)}, f32[2,64,8,512]{3,2,1,0:T(8,128)S(1)}) custom-call(f32[4,64,8,512]{3,2,1,0:T(8,128)} %bitcast.2), custom_call_target="tpu_custom_call" | custom-call | tf_op jit(solution)/shard_map/exchange/pallas_call | solution.py:209
  190.6 2.2 %mix.1 = f32[2,2,64,8,512]{4,3,2,1,0:T(8,128)} custom-call(f32[2,64,8,512]{3,2,1,0:T(8,128)S(1)} %get-tuple-element.7.a_ref, f32[2,64,8,512]{3,2,1,0:T(8,128)S(1)} %get-tuple-element.8.b_ref), custom_call_target="tpu_custom_call" | custom-call | tf_op jit(solution)/shard_map/mix/pallas_call | solution.py:224

commit v3 on v2

--- a/solution.py
+++ b/solution.py
@@ -10,7 +10,8 @@
 MESH = pl.DeviceIdType.MESH
 LANES = 128
 CHUNKS = 4
-Z_ORDER = (4, 3, 5, 2, 6, 1, 7)
+Z_FAR = (4, 3, 5)
+Z_NEAR = (2, 6, 1, 7)
 
 
 def butterfly(values):
@@ -40,7 +41,7 @@
     return high, low
 
 
-def exchange_kernel(n_z, n_y, n_row, x_ref, a_out, b_out, z_in, z_sum, z_back, p_in, p_sum, p_back, local, table, send_sem, recv_sem):
+def exchange_kernel(n_z, n_y, n_row, x_ref, a_out, b_out, z_in, z_sum, z_back, p_in, p_sum, p_back, local, table, send_sem, recv_sem, ready_sem):
     row = lax.axis_index("row")
     col = lax.axis_index("col")
     z = col // n_y
@@ -58,25 +59,34 @@
         k = lax.rem(p + step, n_p)
         return k, (k // n_y, z * n_y + lax.rem(k, n_y))
 
-    barrier = pltpu.get_barrier_semaphore()
-    for step in Z_ORDER:
-        pl.semaphore_signal(barrier, inc=1, device_id=z_peer(step)[1], device_id_type=MESH)
-
-    @pl.loop(1, n_p)
-    def _(step):
-        pl.semaphore_signal(barrier, inc=1, device_id=p_peer(step)[1], device_id_type=MESH)
-
-    pl.semaphore_wait(barrier, n_z - 1 + n_p - 1)
-
-    def z_send(src, dst, slot):
+    x, core = row // 2, lax.rem(row, 2)
+    n_x = n_row // 2
+    neighbours = [z_peer(1)[1], z_peer(n_z - 1)[1]]
+    neighbours += [(row, z * n_y + lax.rem(y + step, n_y)) for step in (1, n_y - 1)]
+    neighbours += [(lax.rem(x + step, n_x) * 2 + core, col) for step in (1, n_x - 1)]
+    neighbours += [(x * 2 + 1 - core, col)]
+
+    def greet(semaphore):
+        for device in neighbours:
+            pl.semaphore_signal(semaphore, inc=1, device_id=device, device_id_type=MESH)
+        pl.semaphore_wait(semaphore, len(neighbours))
+
+    def z_pieces(src, dst, slot, steps):
         mine = pl.ds(z * z_len, z_len)
-        for step in Z_ORDER:
+        for step in steps:
             k, device = z_peer(step)
             pltpu.make_async_remote_copy(
                 src_ref=src.at[pl.ds(k * z_len, z_len)], dst_ref=dst.at[mine],
                 send_sem=send_sem.at[slot], recv_sem=recv_sem.at[slot], device_id=device, device_id_type=MESH,
             ).start()
+
+    def z_own(src, dst, slot):
+        mine = pl.ds(z * z_len, z_len)
         pltpu.make_async_copy(src.at[mine], dst.at[mine], recv_sem.at[slot]).start()
+
+    def z_send(src, dst, slot, near=Z_NEAR):
+        z_pieces(src, dst, slot, Z_FAR + near)
+        z_own(src, dst, slot)
 
     def p_send(src, dst, slot):
         mine = pl.ds(p * p_len, p_len)
@@ -134,8 +144,17 @@
                     dst[chunk, base + t, :, at] = value
 
     a_chunks, b_chunks = (0, 1), (2, 3)
-    for a, b in zip(a_chunks, b_chunks):
-        z_send(x_ref.at[a], z_in.at[a], a)
+    greet(pltpu.get_barrier_semaphore())
+    z_pieces(x_ref.at[0], z_in.at[0], 0, (1, n_z - 1))
+    for hops in (2, 3):
+        greet(ready_sem.at[hops - 2])
+        z_pieces(x_ref.at[0], z_in.at[0], 0, (hops, n_z - hops))
+    greet(ready_sem.at[2])
+    z_pieces(x_ref.at[0], z_in.at[0], 0, (n_z // 2,))
+    z_own(x_ref.at[0], z_in.at[0], 0)
+    z_send(x_ref.at[1], z_in.at[1], 1)
+    greet(ready_sem.at[3])
+    for b in b_chunks:
         p_send(x_ref.at[b], p_in.at[b], 8 + b)
 
     table[...] = signs(lanes, lanes)
@@ -172,7 +191,9 @@
 
     arrived(z_in.at[3], 3)
     combine(z_in.at[3], z_sum.at[3], n_z, z_len)
-    z_send(z_sum.at[3], b_out.at[1], 7)
+    to_first_up = (z + 1) // n_z
+    to_first_down = (lax.rem(z + n_z - 2, n_z) + 1) // n_z
+    z_send(z_sum.at[3], b_out.at[1], 7, (2 - to_first_up, n_z - 2 + to_first_down, 1 + to_first_up, n_z - 1 - to_first_down))
 
     for b in b_chunks:
         arrived(b_out.at[b - 2], 4 + b)
@@ -214,7 +235,7 @@
         scratch_shapes=[
             full, full, half, full, full, full, half,
             pltpu.VMEM((lanes, lanes), jnp.bfloat16),
-            pltpu.SemaphoreType.DMA((4 * CHUNKS,)), pltpu.SemaphoreType.DMA((4 * CHUNKS,)),
+            pltpu.SemaphoreType.DMA((4 * CHUNKS,)), pltpu.SemaphoreType.DMA((4 * CHUNKS,)), pltpu.SemaphoreType.REGULAR((4,)),
         ],
         compiler_params=pltpu.CompilerParams(collective_id=0, has_side_effects=True, vmem_limit_bytes=58 * 2**20),
         name="exchange",

time: 196 us -> 191 us (0.974)
  Pallas kernels: 193 us -> 189 us
    pallas_call x1, Pallas kernels: 191 us -> 186 us  [per_device(): pl.pallas_call(functools.partial(exchange_kernel, n_z, n_y, n_row), out_s...]
where the time goes in v3:
time: 191 us; the launch traced here: 189 us
  Pallas kernels  189 us (99%)
    pallas_call x1, Pallas kernels, per_device(): pl.pallas_call(functools.partial(exchange_kernel, n_z, n_y, n_row), out_s...  186 us

profile of v3, /device:TPU:12, one launch (start us, length us, event | category | flops | bytes accessed | tf_op | source)
XLA Modules:
  0.0 188.7 jit_solution(7012142041853901748)
XLA Ops:
  0.0 186.5 %exchange.1 = (f32[2,64,8,512]{3,2,1,0:T(8,128)S(1)}, f32[2,64,8,512]{3,2,1,0:T(8,128)S(1)}) custom-call(f32[4,64,8,512]{3,2,1,0:T(8,128)} %bitcast.2), custom_call_target="tpu_custom_call" | custom-call | tf_op jit(solution)/shard_map/exchange/pallas_call | solution.py:230
  186.5 2.2 %mix.1 = f32[2,2,64,8,512]{4,3,2,1,0:T(8,128)} custom-call(f32[2,64,8,512]{3,2,1,0:T(8,128)S(1)} %get-tuple-element.7.a_ref, f32[2,64,8,512]{3,2,1,0:T(8,128)S(1)} %get-tuple-element.8.b_ref), custom_call_target="tpu_custom_call" | custom-call | tf_op jit(solution)/shard_map/mix/pallas_call | solution.py:245

commit v4 on v3

--- a/solution.py
+++ b/solution.py
@@ -10,8 +10,8 @@
 MESH = pl.DeviceIdType.MESH
 LANES = 128
 CHUNKS = 4
-Z_FAR = (4, 3, 5)
-Z_NEAR = (2, 6, 1, 7)
+Z_ORDER = (4, 3, 5, 2, 6, 1, 7)
+Z_EARLY = (1, 0, 2, 3)
 
 
 def butterfly(values):
@@ -71,21 +71,28 @@
             pl.semaphore_signal(semaphore, inc=1, device_id=device, device_id_type=MESH)
         pl.semaphore_wait(semaphore, len(neighbours))
 
-    def z_pieces(src, dst, slot, steps):
-        mine = pl.ds(z * z_len, z_len)
-        for step in steps:
-            k, device = z_peer(step)
-            pltpu.make_async_remote_copy(
-                src_ref=src.at[pl.ds(k * z_len, z_len)], dst_ref=dst.at[mine],
-                send_sem=send_sem.at[slot], recv_sem=recv_sem.at[slot], device_id=device, device_id_type=MESH,
-            ).start()
+    def z_piece(src, dst, slot, step):
+        k, device = z_peer(step)
+        pltpu.make_async_remote_copy(
+            src_ref=src.at[pl.ds(k * z_len, z_len)], dst_ref=dst.at[pl.ds(z * z_len, z_len)],
+            send_sem=send_sem.at[slot], recv_sem=recv_sem.at[slot], device_id=device, device_id_type=MESH,
+        ).start()
 
     def z_own(src, dst, slot):
         mine = pl.ds(z * z_len, z_len)
         pltpu.make_async_copy(src.at[mine], dst.at[mine], recv_sem.at[slot]).start()
 
-    def z_send(src, dst, slot, near=Z_NEAR):
-        z_pieces(src, dst, slot, Z_FAR + near)
+    def z_send(src, dst, slot):
+        for step in Z_ORDER:
+            z_piece(src, dst, slot, step)
+        z_own(src, dst, slot)
+
+    def z_send_early(src, dst, slot):
+        for k in Z_EARLY:
+            pl.when(z != k)(functools.partial(z_piece, src, dst, slot, lax.rem(k - z + n_z, n_z)))
+        for step in Z_ORDER:
+            late = lax.rem(z + step, n_z) >= len(Z_EARLY)
+            pl.when(late)(functools.partial(z_piece, src, dst, slot, step))
         z_own(src, dst, slot)
 
     def p_send(src, dst, slot):
@@ -145,12 +152,11 @@
 
     a_chunks, b_chunks = (0, 1), (2, 3)
     greet(pltpu.get_barrier_semaphore())
-    z_pieces(x_ref.at[0], z_in.at[0], 0, (1, n_z - 1))
-    for hops in (2, 3):
-        greet(ready_sem.at[hops - 2])
-        z_pieces(x_ref.at[0], z_in.at[0], 0, (hops, n_z - hops))
-    greet(ready_sem.at[2])
-    z_pieces(x_ref.at[0], z_in.at[0], 0, (n_z // 2,))
+    for hops in range(1, n_z // 2 + 1):
+        if hops > 1:
+            greet(ready_sem.at[hops - 2])
+        for step in sorted({hops, n_z - hops}):
+            z_piece(x_ref.at[0], z_in.at[0], 0, step)
     z_own(x_ref.at[0], z_in.at[0], 0)
     z_send(x_ref.at[1], z_in.at[1], 1)
     greet(ready_sem.at[3])
@@ -191,9 +197,7 @@
 
     arrived(z_in.at[3], 3)
     combine(z_in.at[3], z_sum.at[3], n_z, z_len)
-    to_first_up = (z + 1) // n_z
-    to_first_down = (lax.rem(z + n_z - 2, n_z) + 1) // n_z
-    z_send(z_sum.at[3], b_out.at[1], 7, (2 - to_first_up, n_z - 2 + to_first_down, 1 + to_first_up, n_z - 1 - to_first_down))
+    z_send_early(z_sum.at[3], b_out.at[1], 7)
 
     for b in b_chunks:
         arrived(b_out.at[b - 2], 4 + b)

time: 191 us -> 191 us (level)
  no operation moved by 1% of the time
where the time goes in v4:
time: 191 us; the launch traced here: 188 us
  Pallas kernels  188 us (98%)
    pallas_call x1, Pallas kernels, per_device(): pl.pallas_call(functools.partial(exchange_kernel, n_z, n_y, n_row), out_s...  186 us

profile of v4, /device:TPU:12, one launch (start us, length us, event | category | flops | bytes accessed | tf_op | source)
XLA Modules:
  0.0 188.4 jit_solution(4395069467614460100)
XLA Ops:
  0.0 186.2 %exchange.1 = (f32[2,64,8,512]{3,2,1,0:T(8,128)S(1)}, f32[2,64,8,512]{3,2,1,0:T(8,128)S(1)}) custom-call(f32[4,64,8,512]{3,2,1,0:T(8,128)} %bitcast.2), custom_call_target="tpu_custom_call" | custom-call | tf_op jit(solution)/shard_map/exchange/pallas_call | solution.py:234
  186.2 2.2 %mix.1 = f32[2,2,64,8,512]{4,3,2,1,0:T(8,128)} custom-call(f32[2,64,8,512]{3,2,1,0:T(8,128)S(1)} %get-tuple-element.7.a_ref, f32[2,64,8,512]{3,2,1,0:T(8,128)S(1)} %get-tuple-element.8.b_ref), custom_call_target="tpu_custom_call" | custom-call | tf_op jit(solution)/shard_map/mix/pallas_call | solution.py:249
